TPU v7x, 128 devices: a whole 4x4x4 slice. The times are simulated.
128 devices in a mesh: mu: 16 (over y, z_hi, core), nu: 8 (over z_lo, x).
Axes of the slice: x: 4, y: 4, z: 4 (z_hi: 2, z_lo: 2; z = z_hi * 2 + z_lo), core: 2. Of those that a mesh axis runs over, the one named last changes fastest.
Arguments:
- earlier_vectors: float32 [1024, 1024, 512], P('mu', 'nu'), may hold values from -0.72 to 0.72
- pivot_integral_columns: float32 [1024, 1024, 256], P('mu', 'nu'), may hold values from -6 to 6
- diagonal: float32 [1024, 1024], P('mu', 'nu'), may hold values from 2 to 60
- orbitals: float32 [1024, 40], replicated, may hold values from -0.1875 to 0.1875
- pivots: int32 [256], replicated, may hold values from 0 to 1048575, as said below
Outputs:
- transformed: float32 [256, 820], P(('mu', 'nu'))
- updated_diagonal: float32 [1024, 1024], P('mu', 'nu')
Inputs may be any that keep to these rules, and one draw needn't show every extreme that they name: The pivots are distinct. The pairs held by one device (a block of 64 first by 128 second AO indices) contain at most 8 pivots, and some block contains exactly 8.
All inputs are finite; a program needn't handle non-finite values.
Results may differ from a plain program's by a relative error of at most 0.0001.
Values sent between devices are 32-bit elements; how exact they have to be, the bound alone decides.
No kernel may reach another device: no remote copies, remote signals or barrier semaphores. Data moves between devices by JAX's collectives and lax.ppermute only.
A program may use at most 128 MiB of HBM per device.

v0:
```python
import jax
import jax.numpy as jnp
import numpy as np
from jax import lax
from jax.sharding import PartitionSpec as P

precise = lax.Precision.HIGHEST


def cut_along(value, dim, length):
    dims = value.shape
    pieces = value.reshape(*dims[:dim], length, dims[dim] // length, *dims[dim + 1 :])
    return jnp.moveaxis(pieces, dim, 0)


def summed_on_arrival(value, axis, dim):
    pieces = cut_along(value, dim, lax.axis_size(axis))
    arrived = lax.all_to_all(pieces, axis, split_axis=0, concat_axis=0, tiled=True)
    return arrived.sum(axis=0)


def local(earlier_vectors, pivot_integral_columns, diagonal, orbitals, pivots):
    orbital_rows_mu, cols_nu, preceding = earlier_vectors.shape
    pivot_count = pivots.shape[0]
    ao_count, active = orbitals.shape
    size_mu = lax.axis_size("mu")
    size_nu = lax.axis_size("nu")
    index_mu = lax.axis_index("mu")
    index_nu = lax.axis_index("nu")
    pivot_mu = pivots // ao_count
    pivot_nu = pivots % ao_count
    owner_mu = pivot_mu // orbital_rows_mu
    owner_nu = pivot_nu // cols_nu
    local_row = pivot_mu % orbital_rows_mu * cols_nu + pivot_nu % cols_nu
    is_owned = (owner_mu == index_mu) & (owner_nu == index_nu)
    flat_vectors = earlier_vectors.reshape(orbital_rows_mu * cols_nu, preceding)
    flat_diag = diagonal.reshape(orbital_rows_mu * cols_nu)
    picked = jnp.take(flat_vectors, local_row, axis=0)
    picked_diag = jnp.take(flat_diag, local_row)
    masked = jnp.where(is_owned[:, None], picked, 0.0)
    masked_diag = jnp.where(is_owned, picked_diag, 0.0)
    pivot_rows, pivot_diag = lax.psum((masked, masked_diag), ("mu", "nu"))
    residual_diag = pivot_diag - jnp.sum(pivot_rows * pivot_rows, axis=1)
    scaling = lax.rsqrt(jnp.maximum(residual_diag, 1.0))
    update = lax.dot_general(flat_vectors, pivot_rows, (((1,), (1,)), ((), ())), precision=precise)
    flat_columns = pivot_integral_columns.reshape(orbital_rows_mu * cols_nu, pivot_count)
    fresh_vectors = (flat_columns - update) * scaling[None, :]
    updated_diagonal = (flat_diag - jnp.sum(fresh_vectors * fresh_vectors, axis=1)).reshape(
        orbital_rows_mu, cols_nu
    )
    basis_left_index = lax.dynamic_slice_in_dim(
        orbitals, index_mu * orbital_rows_mu, orbital_rows_mu, 0
    )
    orbit_nu = lax.dynamic_slice_in_dim(orbitals, index_nu * cols_nu, cols_nu, 0)
    fresh_blocks = fresh_vectors.reshape(orbital_rows_mu, cols_nu, pivot_count)
    half_done = jnp.einsum("mp,mnj->jpn", basis_left_index, fresh_blocks, precision=precise)
    row_index, col_index = np.tril_indices(active)
    full_done = jnp.einsum("nq,jpn->jpq", orbit_nu, half_done, precision=precise)
    pair_values = full_done[:, row_index, col_index]
    pair_count = row_index.shape[0]
    per_device = pivot_count // (size_mu * size_nu)
    split_mu = pair_values.reshape(size_mu, size_nu * per_device, pair_count)
    summed = summed_on_arrival(split_mu, "mu", 0)
    split_nu = summed.reshape(size_nu, per_device, pair_count)
    transformed = summed_on_arrival(split_nu, "nu", 0).reshape(per_device, pair_count)
    return (transformed, updated_diagonal)


def solution(mesh):
    placed = (P("mu", "nu", None), P("mu", "nu", None), P("mu", "nu"), P(), P())
    return jax.shard_map(
        local,
        mesh=mesh,
        in_specs=placed,
        out_specs=(P(("mu", "nu"), None), P("mu", "nu")),
        check_vma=False,
    )
```

profile of v0, /device:TPU:0, one launch (start us, length us, event | category | flops | bytes accessed | tf_op | source)
XLA Modules:
  0.0 257.5 jit_solution(8230308428707092736)
XLA Ops:
  7.2 0.0 all-reduce.2.cloned.1.call-start
  7.2 0.7 compare_select_fusion
  8.0 2.0 gather_fusion.1
  10.0 7.0 %gather_fusion = f32[256,512]{1,0:T(8,128)S(1)} fusion(f32[8192,512]{1,0:T(8,128)} %bitcast.34, s32[1024]{0:T(1024)S(1)} %pad_clamp_fusion), kind=kCustom, calls=%fused_computation | custom fusion | bytes 1049600 | tf_op jit(solution)/shard_map/jit(_take)/gather | solution.py:38
  17.0 0.7 select_select_fusion.1
  17.7 1.0 select_select_fusion
  18.7 8.9 %copy.20 = f32[8192,256]{0,1:T(8,128)} copy(f32[8192,256]{1,0:T(8,128)} %bitcast.36) | data formatting | bytes 16777216 | tf_op jit(solution)/shard_map/reshape | solution.py:46
  27.6 69.1 %psum.15 = f32[256]{0:T(256)S(1)} all-reduce(f32[256]{0:T(256)S(1)} %get-tuple-element.2), channel_id=1, replica_groups=mesh['mu'=16,'nu'=8] {'mu','nu'}, use_global_device_ids=true, to_apply=%region_1.2 | all-reduce | flops 256 | bytes 2048 | tf_op jit(solution)/shard_map/psum | solution.py:42
  96.8 69.2 %all-reduce.2.cloned.1.call-done = f32[256,512]{1,0:T(8,128)} async-done(((f32[256,512]{1,0:T(8,128)}), f32[256,512]{1,0:T(8,128)}) %all-reduce.2.cloned.1.call-update) | async-done | bytes 524304 | tf_op jit(solution)/shard_map/psum | solution.py:42
  166.0 1.2 multiply_reduce_fusion.1
  167.1 19.7 %multiply_reduce_fusion = (f32[8192]{0:T(1024)S(1)}, f32[8192,256]{0,1:T(8,128)S(1)}) fusion(f32[256]{0:T(256)S(1)} %maximum_rsqrt_fusion, f32[8192,256]{0,1:T(8,128)} %copy.20, f32[256,512]{1,0:T(8,128)} %all-reduce.2.cloned.1.call-done, f32[8192,512]{1,0:T(8,128)} %bitcast.35), kind=kOutput, calls=%fused_computation.6 | convolution fusion | flops 12893282304 | bytes 34112512 | tf_op jit(solution)/shard_map/dot_general | solution.py:45
  186.9 1.6 copy.21
  188.6 6.6 %fusion.5 = f32[128,256,40]{0,2,1:T(8,128)S(1)} fusion(f32[64,128,256]{1,0,2:T(8,128)S(1)} %bitcast.32, f32[1024,40]{0,1:T(8,128)S(1)} %copy-done, s32[]{:T(128)S(6)} %select_n.71), kind=kOutput, calls=%fused_computation.13 | convolution fusion | flops 1006632960 | bytes 13651972 | tf_op jit(solution)/shard_map/mp,mnj->jpn/dot_general | solution.py:56
  195.2 5.9 %fusion.2 = f32[256,40,40]{2,1,0:T(8,128)} fusion(f32[128,256,40]{0,2,1:T(8,128)S(1)} %fusion.5, f32[1024,40]{0,1:T(8,128)S(1)} %copy-done, s32[]{:T(128)S(6)} %select_n.72), kind=kOutput, calls=%fused_computation.7 | convolution fusion | flops 629145600 | bytes 6901764 | tf_op jit(solution)/shard_map/nq,jpn->jpq/dot_general | solution.py:58
  201.1 5.0 %copy.19 = f32[256,40,40]{0,2,1:T(8,128)S(1)} copy(f32[256,40,40]{2,1,0:T(8,128)} %fusion.2) | data formatting | bytes 3276800 | tf_op jit(solution)/shard_map/nq,jpn->jpq/dot_general | solution.py:58
  206.2 11.0 %gather_fusion.2 = f32[820,256]{1,0:T(8,128)S(1)} fusion(f32[256,40,40]{0,2,1:T(8,128)S(1)} %copy.19, s32[820]{0:T(1024)S(1)} %copy-done.1), kind=kCustom, calls=%fused_computation.2 | custom fusion | bytes 1685920 | tf_op jit(solution)/shard_map/gather | solution.py:59
  217.1 0.3 copy.16
  217.4 21.5 %all_to_all.10 = f32[16,1,16,820]{3,2,1,0:T(8,128)S(1)} all-to-all(f32[16,1,16,820]{3,2,1,0:T(8,128)S(1)} %bitcast.38), channel_id=1, replica_groups=mesh['mu'=16,'nu'=8] {'mu'}, dimensions={0} | all-to-all | bytes 1679360 | tf_op jit(solution)/shard_map/all_to_all | solution.py:18
  239.0 0.1 reduce_sum.39
  239.0 0.7 reshape_reshape.7
  239.7 4.0 %all-to-all-start.1 = ((f32[8,1,2,820]{3,2,1,0:T(2,128)}), f32[8,1,2,820]{3,2,1,0:T(2,128)S(1)}, u32[]{:S(2)}, u32[]{:S(2)}) async-start(f32[8,1,2,820]{3,2,1,0:T(2,128)} %reshape_reshape.7), calls=%async_computation.1 | async-start | bytes 114688 | tf_op jit(solution)/shard_map/all_to_all | solution.py:18
  243.7 0.6 bitcast_subtract_fusion
  244.4 5.7 %all-to-all-done.1 = f32[8,1,2,820]{3,2,1,0:T(2,128)S(1)} async-done(((f32[8,1,2,820]{3,2,1,0:T(2,128)}), f32[8,1,2,820]{3,2,1,0:T(2,128)S(1)}, u32[]{:S(2)}, u32[]{:S(2)}) %all-to-all-start.1) | async-done | bytes 52512 | tf_op jit(solution)/shard_map/all_to_all | solution.py:18
  250.1 0.6 reduce_sum.40
  (9 shorter events, 0.1 us)
Async XLA Ops:
  7.2 181.4 %copy-start = (f32[1024,40]{0,1:T(8,128)S(1)}, f32[1024,40]{0,1:T(8,128)}, u32[]{:S(2)}) copy-start(f32[1024,40]{0,1:T(8,128)} %param.12) | copy-start | bytes 491524
  7.2 158.8 %all-reduce.2.cloned.1.call-start = ((), (), s32[]{:S(2)}) async-start(), calls=%async_computation.2 | async-start | bytes 1048576 | tf_op jit(solution)/shard_map/psum | solution.py:42
  195.2 11.0 %copy-start.1 = (s32[820]{0:T(1024)S(1)}, s32[820]{0:T(1024)}, u32[]{:S(2)}) copy-start(s32[820]{0:T(1024)} %constant.144) | copy-start | bytes 9844
  206.1 37.6 %copy-start.2 = (f32[64,128]{1,0:T(8,128)S(1)}, f32[64,128]{1,0:T(8,128)}, u32[]{:S(2)}) copy-start(f32[64,128]{1,0:T(8,128)} %param.11) | copy-start | bytes 98308
  239.7 10.4 %all-to-all-start.1 = ((f32[8,1,2,820]{3,2,1,0:T(2,128)}), f32[8,1,2,820]{3,2,1,0:T(2,128)S(1)}, u32[]{:S(2)}, u32[]{:S(2)}) async-start(f32[8,1,2,820]{3,2,1,0:T(2,128)} %reshape_reshape.7), calls=%async_computation.1 | async-start | bytes 114688 | tf_op jit(solution)/shard_map/all_to_all | solution.py:18
Sparse Core Ops, SparseCore 0:
  18.8 147.1 all-reduce.1
where the time goes:
time: 258 us
  blocking collectives  90.7 us (35%)
  waiting for transfers between devices  74.9 us (29%)
  local copies, waits for them, and re-layouts  36.5 us (14%)
  matrix products  32.3 us (13%)
  between operations  14.1 us (5%)
  other arithmetic  4.92 us (2%)
  starting transfers between devices  4.07 us (2%)
    psum x1, waiting for transfers between devices, local(): pivot_rows, pivot_diag = lax.psum((masked, masked_diag), ('mu', 'nu'))  69.2 us
    psum x1, blocking collectives, local(): pivot_rows, pivot_diag = lax.psum((masked, masked_diag), ('mu', 'nu'))  69.1 us
    all_to_all x1, blocking collectives, summed_on_arrival(): lax.all_to_all(pieces, axis, split_axis=0, concat_axis=0, tiled=True)  21.5 us
    dot_general x1, matrix products, local(): lax.dot_general(flat_vectors, pivot_rows, (((1,), (1,)), ((), ())), preci...  19.7 us
    gather x2, local copies, waits for them, and re-layouts, local(): pair_values = full_done[:, row_index, col_index]  11.3 us
    reshape x1, local copies, waits for them, and re-layouts, local(): pivot_integral_columns.reshape(orbital_rows_mu * cols_nu, pivot_count)  8.94 us
    gather x1, local copies, waits for them, and re-layouts, local(): picked = jnp.take(flat_vectors, local_row, axis=0)  6.98 us
    dot_general x1, matrix products, local(): jnp.einsum('mp,mnj->jpn', basis_left_index, fresh_blocks, precision=precise)  6.61 us
  transfers between devices with their start and end apart: 2, of which 2 were waited for; matrix products, arithmetic and copies ran while one was open for 4% of the time, Pallas kernels for 0%

commit v1 on v0

--- a/solution.py
+++ b/solution.py
@@ -3,8 +3,10 @@
 import numpy as np
 from jax import lax
 from jax.sharding import PartitionSpec as P
+from jax.lax import psum
 
 precise = lax.Precision.HIGHEST
+body_assign = lambda x_local: psum(psum(x_local, axis_name="mu"), axis_name="nu")
 
 
 def cut_along(value, dim, length):
@@ -39,7 +41,7 @@
     picked_diag = jnp.take(flat_diag, local_row)
     masked = jnp.where(is_owned[:, None], picked, 0.0)
     masked_diag = jnp.where(is_owned, picked_diag, 0.0)
-    pivot_rows, pivot_diag = lax.psum((masked, masked_diag), ("mu", "nu"))
+    pivot_rows, pivot_diag = body_assign((masked, masked_diag))
     residual_diag = pivot_diag - jnp.sum(pivot_rows * pivot_rows, axis=1)
     scaling = lax.rsqrt(jnp.maximum(residual_diag, 1.0))
     update = lax.dot_general(flat_vectors, pivot_rows, (((1,), (1,)), ((), ())), precision=precise)

time: 258 us -> 331 us (1.28)
  waiting for transfers between devices: 74.9 us -> 159 us
  blocking collectives: 90.7 us -> 79.9 us
    psum x1 -> x2, waiting for transfers between devices: 69.2 us -> 154 us  [the longest x1 141 us: psum(x_local, axis_name='mu')]
    psum x1 -> x2, blocking collectives: 69.1 us -> 57.1 us  [the longest x1 38.4 us: psum(x_local, axis_name='mu')]
  transfers between devices with their start and end apart: 2 -> 3, of which waited for: 2 -> 3; matrix products, arithmetic and copies ran while one was open for 4% -> 3% of each run, Pallas kernels for 0% -> 0%
where the time goes in v1:
time: 331 us
  waiting for transfers between devices  159 us (48%)
  blocking collectives  79.9 us (24%)
  local copies, waits for them, and re-layouts  36.5 us (11%)
  matrix products  32.3 us (10%)
  between operations  14.2 us (4%)
  other arithmetic  4.83 us (1%)
  starting transfers between devices  3.43 us (1%)
    psum x1, waiting for transfers between devices, psum(x_local, axis_name='mu')  141 us
    psum x1, blocking collectives, psum(x_local, axis_name='mu')  38.4 us
    all_to_all x1, blocking collectives, summed_on_arrival(): lax.all_to_all(pieces, axis, split_axis=0, concat_axis=0, tiled=True)  22.8 us
    dot_general x1, matrix products, local(): lax.dot_general(flat_vectors, pivot_rows, (((1,), (1,)), ((), ())), preci...  19.7 us
    psum x1, blocking collectives, psum(psum(x_local, axis_name='mu'), axis_name='nu')  18.8 us
    psum x1, waiting for transfers between devices, psum(psum(x_local, axis_name='mu'), axis_name='nu')  12.4 us
    gather x2, local copies, waits for them, and re-layouts, local(): pair_values = full_done[:, row_index, col_index]  11.3 us
    reshape x1, local copies, waits for them, and re-layouts, local(): pivot_integral_columns.reshape(orbital_rows_mu * cols_nu, pivot_count)  8.94 us
  transfers between devices with their start and end apart: 3, of which 3 were waited for; matrix products, arithmetic and copies ran while one was open for 3% of the time, Pallas kernels for 0%

profile of v1, /device:TPU:0, one launch (start us, length us, event | category | flops | bytes accessed | tf_op | source)
XLA Modules:
  0.0 330.5 jit_solution(11846429407812418026)
XLA Ops:
  7.2 0.7 compare_select_fusion
  8.0 2.0 gather_fusion.1
  10.0 7.0 %gather_fusion = f32[256,512]{1,0:T(8,128)S(1)} fusion(f32[8192,512]{1,0:T(8,128)} %bitcast.34, s32[1024]{0:T(1024)S(1)} %pad_clamp_fusion), kind=kCustom, calls=%fused_computation | custom fusion | bytes 1049600 | tf_op jit(solution)/shard_map/jit(_take)/gather | solution.py:40
  17.0 0.7 select_select_fusion.1
  17.7 0.9 select_select_fusion
  18.7 141.3 %all-reduce.3.cloned.1.call-done = f32[256,512]{1,0:T(8,128)} async-done(((f32[256,512]{1,0:T(8,128)}), f32[256,512]{1,0:T(8,128)}) %all-reduce.3.cloned.1.call-update) | async-done | bytes 524304 | tf_op jit(solution)/shard_map/psum | solution.py:9
  160.0 8.9 %copy.20 = f32[8192,256]{0,1:T(8,128)} copy(f32[8192,256]{1,0:T(8,128)} %bitcast.36) | data formatting | bytes 16777216 | tf_op jit(solution)/shard_map/reshape | solution.py:48
  168.9 38.4 %psum.30 = f32[256]{0:T(256)S(1)} all-reduce(f32[256]{0:T(256)S(1)} %get-tuple-element.2), channel_id=1, replica_groups=mesh['mu'=16,'nu'=8] {'mu'}, use_global_device_ids=true, to_apply=%region_2.3 | all-reduce | flops 256 | bytes 2048 | tf_op jit(solution)/shard_map/psum | solution.py:9
  207.3 18.8 %psum.31 = f32[256]{0:T(256)S(1)} all-reduce(f32[256]{0:T(256)S(1)} %psum.30), channel_id=1, replica_groups=mesh['mu'=16,'nu'=8] {'nu'}, use_global_device_ids=true, to_apply=%region_3.4 | all-reduce | flops 256 | bytes 2048 | tf_op jit(solution)/shard_map/psum | solution.py:9
  226.1 12.4 %all-reduce.5.cloned.1.call-done = f32[256,512]{1,0:T(8,128)} async-done(((f32[256,512]{1,0:T(8,128)}), f32[256,512]{1,0:T(8,128)}) %all-reduce.5.cloned.1.call-update) | async-done | bytes 524304 | tf_op jit(solution)/shard_map/psum | solution.py:9
  238.5 1.2 multiply_reduce_fusion.1
  239.6 19.7 %multiply_reduce_fusion = (f32[8192]{0:T(1024)S(1)}, f32[8192,256]{0,1:T(8,128)S(1)}) fusion(f32[256]{0:T(256)S(1)} %maximum_rsqrt_fusion, f32[8192,256]{0,1:T(8,128)} %copy.20, f32[256,512]{1,0:T(8,128)} %all-reduce.5.cloned.1.call-done, f32[8192,512]{1,0:T(8,128)} %bitcast.35), kind=kOutput, calls=%fused_computation.6 | convolution fusion | flops 12893282304 | bytes 34112512 | tf_op jit(solution)/shard_map/dot_general | solution.py:47
  259.4 1.6 copy.21
  261.0 6.6 %fusion.5 = f32[128,256,40]{0,2,1:T(8,128)S(1)} fusion(f32[64,128,256]{1,0,2:T(8,128)S(1)} %bitcast.32, f32[1024,40]{0,1:T(8,128)S(1)} %copy-done, s32[]{:T(128)S(6)} %select_n.71), kind=kOutput, calls=%fused_computation.13 | convolution fusion | flops 1006632960 | bytes 13651972 | tf_op jit(solution)/shard_map/mp,mnj->jpn/dot_general | solution.py:58
  267.7 5.9 %fusion.2 = f32[256,40,40]{2,1,0:T(8,128)} fusion(f32[128,256,40]{0,2,1:T(8,128)S(1)} %fusion.5, f32[1024,40]{0,1:T(8,128)S(1)} %copy-done, s32[]{:T(128)S(6)} %select_n.72), kind=kOutput, calls=%fused_computation.7 | convolution fusion | flops 629145600 | bytes 6901764 | tf_op jit(solution)/shard_map/nq,jpn->jpq/dot_general | solution.py:60
  273.6 5.0 %copy.19 = f32[256,40,40]{0,2,1:T(8,128)S(1)} copy(f32[256,40,40]{2,1,0:T(8,128)} %fusion.2) | data formatting | bytes 3276800 | tf_op jit(solution)/shard_map/nq,jpn->jpq/dot_general | solution.py:60
  278.6 11.0 %gather_fusion.2 = f32[820,256]{1,0:T(8,128)S(1)} fusion(f32[256,40,40]{0,2,1:T(8,128)S(1)} %copy.19, s32[820]{0:T(1024)S(1)} %copy-done.1), kind=kCustom, calls=%fused_computation.2 | custom fusion | bytes 1685920 | tf_op jit(solution)/shard_map/gather | solution.py:61
  289.6 0.3 copy.16
  289.9 22.8 %all_to_all.10 = f32[16,1,16,820]{3,2,1,0:T(8,128)S(1)} all-to-all(f32[16,1,16,820]{3,2,1,0:T(8,128)S(1)} %bitcast.38), channel_id=1, replica_groups=mesh['mu'=16,'nu'=8] {'mu'}, dimensions={0} | all-to-all | bytes 1679360 | tf_op jit(solution)/shard_map/all_to_all | solution.py:20
  312.8 0.7 reshape_reshape.7
  313.5 3.3 %all-to-all-start.1 = ((f32[8,1,2,820]{3,2,1,0:T(2,128)}), f32[8,1,2,820]{3,2,1,0:T(2,128)S(1)}, u32[]{:S(2)}, u32[]{:S(2)}) async-start(f32[8,1,2,820]{3,2,1,0:T(2,128)} %reshape_reshape.7), calls=%async_computation.1 | async-start | bytes 114688 | tf_op jit(solution)/shard_map/all_to_all | solution.py:20
  316.8 0.6 bitcast_subtract_fusion
  317.4 5.6 %all-to-all-done.1 = f32[8,1,2,820]{3,2,1,0:T(2,128)S(1)} async-done(((f32[8,1,2,820]{3,2,1,0:T(2,128)}), f32[8,1,2,820]{3,2,1,0:T(2,128)S(1)}, u32[]{:S(2)}, u32[]{:S(2)}) %all-to-all-start.1) | async-done | bytes 52512 | tf_op jit(solution)/shard_map/all_to_all | solution.py:20
  323.1 0.6 reduce_sum.40
  (13 shorter events, 0.2 us)
Async XLA Ops:
  7.2 253.9 %copy-start = (f32[1024,40]{0,1:T(8,128)S(1)}, f32[1024,40]{0,1:T(8,128)}, u32[]{:S(2)}) copy-start(f32[1024,40]{0,1:T(8,128)} %param.12) | copy-start | bytes 491524
  7.2 152.8 %all-reduce.3.cloned.1.call-start = ((), (), s32[]{:S(2)}) async-start(), calls=%async_computation.2 | async-start | bytes 1048576 | tf_op jit(solution)/shard_map/psum | solution.py:9
  18.6 219.8 %all-reduce.5.cloned.1.call-start = ((), (), s32[]{:S(2)}) async-start(), calls=%async_computation.3 | async-start | bytes 1048576 | tf_op jit(solution)/shard_map/psum | solution.py:9
  267.7 11.0 %copy-start.1 = (s32[820]{0:T(1024)S(1)}, s32[820]{0:T(1024)}, u32[]{:S(2)}) copy-start(s32[820]{0:T(1024)} %constant.144) | copy-start | bytes 9844
  278.6 38.2 %copy-start.2 = (f32[64,128]{1,0:T(8,128)S(1)}, f32[64,128]{1,0:T(8,128)}, u32[]{:S(2)}) copy-start(f32[64,128]{1,0:T(8,128)} %param.11) | copy-start | bytes 98308
  313.5 9.6 %all-to-all-start.1 = ((f32[8,1,2,820]{3,2,1,0:T(2,128)}), f32[8,1,2,820]{3,2,1,0:T(2,128)S(1)}, u32[]{:S(2)}, u32[]{:S(2)}) async-start(f32[8,1,2,820]{3,2,1,0:T(2,128)} %reshape_reshape.7), calls=%async_computation.1 | async-start | bytes 114688 | tf_op jit(solution)/shard_map/all_to_all | solution.py:20
Sparse Core Ops, SparseCore 0:
  18.7 141.1 all-reduce.2
  162.6 75.8 all-reduce.4
